TPU v7x, 256 devices: a whole 4x4x8 slice. The times are simulated.
256 devices in a mesh: fsdp: 32 (over z, x_hi, core), tp: 8 (over x_lo, y).
Axes of the slice: x: 4 (x_hi: 2, x_lo: 2; x = x_hi * 2 + x_lo), y: 4, z: 8, core: 2. Of those that a mesh axis runs over, the one named last changes fastest.
Arguments:
- grad_iterate: bfloat16 [3584, 18432], P('tp', 'fsdp'), may hold values from -0.036828478 to 0.036828478
Outputs:
- update: float32 [3584, 18432], P('tp', 'fsdp')
All inputs are finite; a program needn't handle non-finite values.
Results may differ from a plain program's by a relative error of at most 0.0031.
Values may be sent and summed in bfloat16 or wider, within the bound.
No kernel may reach another device: no remote copies, remote signals or barrier semaphores. Data moves between devices by JAX's collectives and lax.ppermute only.
A program may use at most 64 MiB of HBM per device.

v0:
```python
import math

import jax
import jax.numpy as jnp
from jax import lax
from jax.sharding import PartitionSpec as P

C = 18432


quintic_one = 3.4445
quintic_three = -4.775
quintic_five = 2.0315


def local(grad_iterate):
    columns = lax.all_gather(grad_iterate, "tp", axis=0, tiled=True)
    partial_value = lax.dot_general(
        grad_iterate, columns, (((1,), (1,)), ((), ())), preferred_element_type=jnp.float32
    )
    gram_low = lax.psum(partial_value, "fsdp").astype(jnp.bfloat16)
    applied = jnp.dot(gram_low, columns, preferred_element_type=jnp.float32)
    applied_low = applied.astype(jnp.bfloat16)
    twice_applied = jnp.dot(
        gram_low,
        lax.all_gather(applied_low, "tp", axis=0, tiled=True),
        preferred_element_type=jnp.float32,
    )
    mixed = (
        quintic_one * grad_iterate.astype(jnp.float32)
        + quintic_three * applied
        + quintic_five * twice_applied
    )
    return mixed * math.sqrt(C)


def solution(mesh):
    return jax.shard_map(
        local,
        mesh=mesh,
        in_specs=(P("tp", "fsdp"),),
        out_specs=P("tp", "fsdp"),
        check_vma=False,
    )
```

profile of v0, /device:TPU:32, one launch (start us, length us, event | category | flops | bytes accessed | tf_op | source)
XLA Modules:
  0.0 324.6 jit_solution(7680048696813712530)
XLA Ops:
  6.5 0.0 all-gather.3.cloned.1.call-start
  6.5 0.7 all-gather.3.cloned.1.call-update
  7.3 0.0 all-gather.5.cloned.1.call-start
  7.3 63.3 %all-gather.3.cloned.1.call-done = bf16[3584,576]{1,0:T(8,128)(2,1)} async-done(((bf16[448,576]{1,0:T(8,128)(2,1)}), bf16[3584,576]{1,0:T(8,128)(2,1)}) %all-gather.3.cloned.1.call-update) | async-done | bytes 4128784 | tf_op jit(solution)/shard_map/all_gather | solution.py:17
  70.6 7.9 %fusion.14 = f32[448,3584]{1,0:T(8,128)} fusion(bf16[448,576]{1,0:T(8,128)(2,1)} %param.1, bf16[3584,576]{1,0:T(8,128)(2,1)} %all-gather.3.cloned.1.call-done), kind=kOutput, calls=%fused_computation.8 | convolution fusion | flops 1849688064 | bytes 11067392 | tf_op jit(solution)/shard_map/dot_general | solution.py:18
  78.5 158.5 %all-reduce.1 = bf16[448,3584]{1,0:T(8,128)(2,1)S(1)} all-reduce(f32[448,3584]{1,0:T(8,128)} %fusion.14), channel_id=1, replica_groups=mesh['fsdp'=32,'tp'=8] {'fsdp'}, use_global_device_ids=true, to_apply=%region_0.0 | all-reduce | flops 1605632 | bytes 9633792 | tf_op jit(solution)/shard_map/psum | solution.py:21
  237.0 6.2 %fusion.13 = (bf16[448,576]{1,0:T(8,128)(2,1)}, f32[448,576]{1,0:T(8,128)}) fusion(bf16[448,3584]{1,0:T(8,128)(2,1)S(1)} %all-reduce.1, bf16[3584,576]{1,0:T(8,128)(2,1)} %all-gather.3.cloned.1.call-done), kind=kOutput, calls=%fused_computation.7 | convolution fusion | flops 1849946112 | bytes 8888320 | tf_op jit(solution)/shard_map/dot_general | solution.py:22
  243.2 0.0 all-gather.5.cloned.1.call-update
  243.2 68.1 %all-gather.5.cloned.1.call-done = bf16[3584,576]{1,0:T(8,128)(2,1)} async-done(((bf16[448,576]{1,0:T(8,128)(2,1)}), bf16[3584,576]{1,0:T(8,128)(2,1)}) %all-gather.5.cloned.1.call-update) | async-done | bytes 4128784 | tf_op jit(solution)/shard_map/all_gather | solution.py:26
  311.3 6.5 %fusion.10 = f32[448,576]{1,0:T(8,128)} fusion(bf16[3584,576]{1,0:T(8,128)(2,1)} %all-gather.5.cloned.1.call-done, bf16[448,3584]{1,0:T(8,128)(2,1)S(1)} %all-reduce.1, f32[448,576]{1,0:T(8,128)} %get-tuple-element.6, bf16[448,576]{1,0:T(8,128)(2,1)} %param.1), kind=kOutput, calls=%fused_computation.6 | convolution fusion | flops 1851494400 | bytes 9920512 | tf_op jit(solution)/shard_map/dot_general | solution.py:24
Async XLA Ops:
  6.5 64.1 %all-gather.3.cloned.1.call-start = ((), (), s32[]{:S(2)}) async-start(), calls=%async_computation | async-start | bytes 5160960 | tf_op jit(solution)/shard_map/all_gather | solution.py:17
  7.3 304.0 %all-gather.5.cloned.1.call-start = ((), (), s32[]{:S(2)}) async-start(), calls=%async_computation.1 | async-start | bytes 5160960 | tf_op jit(solution)/shard_map/all_gather | solution.py:26
Sparse Core Ops, SparseCore 0:
  9.1 61.4 all-gather.2
  243.3 67.9 all-gather.4
where the time goes:
time: 326 us; the launch traced here: 325 us
  blocking collectives  158 us (48%)
  waiting for transfers between devices  132 us (40%)
  matrix products  20.5 us (6%)
  between operations  13.4 us (4%)
    psum x1, blocking collectives, local(): gram_low = lax.psum(partial_value, 'fsdp').astype(jnp.bfloat16)  158 us
    all_gather x1, waiting for transfers between devices, local(): lax.all_gather(applied_low, 'tp', axis=0, tiled=True)  68.1 us
    all_gather x1, waiting for transfers between devices, local(): columns = lax.all_gather(grad_iterate, 'tp', axis=0, tiled=True)  63.3 us
    dot_general x1, matrix products, local(): lax.dot_general(grad_iterate, columns, (((1,), (1,)), ((), ())), preferre...  7.87 us
  transfers between devices with their start and end apart: 2, of which 2 were waited for; matrix products, arithmetic and copies ran while one was open for 0% of the time, Pallas kernels for 0%

commit v1 on v0

v1 whole, which is shorter than its diff:
```python
import math

import jax
import jax.numpy as jnp
from jax import lax
from jax.sharding import Mesh, PartitionSpec as P

C = 18432


quintic_one = 3.4445
quintic_three = -4.775
quintic_five = 2.0315

TP = ("x_lo", "y")
SWAP = [(0, 1), (1, 0)]


def dot(a, b, dims):
    return lax.dot_general(a, b, (dims, ((), ())), preferred_element_type=jnp.float32)


def local(x):
    core = lax.axis_index("core")
    columns = lax.all_gather(x, TP, axis=0, tiled=True)
    half = columns.shape[0] // 2
    mine = lax.dynamic_slice_in_dim(columns, core * half, half, 0)
    other = lax.dynamic_slice_in_dim(columns, (1 - core) * half, half, 0)
    got = lax.ppermute(dot(x, other, ((1,), (1,))), "core", SWAP)
    pair = dot(x, mine, ((1,), (1,))) + got
    rows = lax.psum_scatter(pair, "z", scatter_dimension=0, tiled=True)
    rows = rows + lax.ppermute(rows, "x_hi", SWAP)
    gram_mine = lax.all_gather(rows.astype(jnp.bfloat16), "z", axis=0, tiled=True)
    gram_other = lax.ppermute(gram_mine, "core", SWAP)
    applied = dot(gram_mine, mine, ((1,), (0,))) + dot(gram_other, other, ((1,), (0,)))
    applied_all = lax.all_gather(applied.astype(jnp.bfloat16), TP, axis=0, tiled=True)
    applied_mine = lax.dynamic_slice_in_dim(applied_all, core * half, half, 0)
    applied_other = lax.dynamic_slice_in_dim(applied_all, (1 - core) * half, half, 0)
    twice_applied = dot(gram_mine, applied_mine, ((1,), (0,))) + dot(
        gram_other, applied_other, ((1,), (0,))
    )
    mixed = (
        quintic_one * x.astype(jnp.float32)
        + quintic_three * applied
        + quintic_five * twice_applied
    )
    return mixed * math.sqrt(C)


def solution(mesh):
    grid = Mesh(mesh.devices.reshape(8, 2, 2, 2, 4), ("z", "x_hi", "core", "x_lo", "y"))
    spec = P(TP, ("z", "x_hi", "core"))
    return jax.shard_map(local, mesh=grid, in_specs=(spec,), out_specs=spec, check_vma=False)
```

time: 326 us -> 266 us (0.82)
  blocking collectives: 158 us -> 0 us
  waiting for transfers between devices: 132 us -> 225 us
    psum x1 -> x0, blocking collectives: 158 us -> none  [local(): gram_low = lax.psum(partial_value, 'fsdp').astype(jnp.bfloat16)]
    reduce_scatter x0 -> x1, waiting for transfers between devices: none -> 45.2 us  [local(): rows = lax.psum_scatter(pair, 'z', scatter_dimension=0, tiled=True)]
    all_gather x2 -> x3, waiting for transfers between devices: 131 us -> 162 us  [the longest x1 63.3 us: local(): columns = lax.all_gather(x, TP, axis=0, tiled=True)]
    ppermute x0 -> x3, waiting for transfers between devices: none -> 16.7 us  [the longest x1 7.09 us: local(): rows = rows + lax.ppermute(rows, 'x_hi', SWAP)]
    dot_general x3 -> x6, matrix products: 20.5 us -> 21.9 us  [dot(): lax.dot_general(a, b, (dims, ((), ())), preferred_element_type=jnp.float32)]
  transfers between devices with their start and end apart: 2 -> 7, of which waited for: 2 -> 7; matrix products, arithmetic and copies ran while one was open for 0% -> 0% of each run, Pallas kernels for 0% -> 0%
where the time goes in v1:
time: 266 us; the launch traced here: 264 us
  waiting for transfers between devices  225 us (85%)
  matrix products  21.9 us (8%)
  between operations  13.2 us (5%)
  starting transfers between devices  3.08 us (1%)
    all_gather x1, waiting for transfers between devices, local(): columns = lax.all_gather(x, TP, axis=0, tiled=True)  63.3 us
    all_gather x1, waiting for transfers between devices, local(): lax.all_gather(applied.astype(jnp.bfloat16), TP, axis=0, tiled=True)  57.9 us
    reduce_scatter x1, waiting for transfers between devices, local(): rows = lax.psum_scatter(pair, 'z', scatter_dimension=0, tiled=True)  45.2 us
    all_gather x1, waiting for transfers between devices, local(): lax.all_gather(rows.astype(jnp.bfloat16), 'z', axis=0, tiled=True)  40.6 us
    dot_general x6, matrix products, dot(): lax.dot_general(a, b, (dims, ((), ())), preferred_element_type=jnp.float32)  21.9 us
    ppermute x1, waiting for transfers between devices, local(): rows = rows + lax.ppermute(rows, 'x_hi', SWAP)  7.09 us
    ppermute x1, waiting for transfers between devices, local(): got = lax.ppermute(dot(x, other, ((1,), (1,))), 'core', SWAP)  5.96 us
  transfers between devices with their start and end apart: 7, of which 7 were waited for; matrix products, arithmetic and copies ran while one was open for 0% of the time, Pallas kernels for 0%

profile of v1, /device:TPU:32, one launch (start us, length us, event | category | flops | bytes accessed | tf_op | source)
XLA Modules:
  0.0 264.4 jit_solution(11842380710855404378)
XLA Ops:
  6.5 0.7 all-gather.4.cloned.1.call-update
  7.3 0.0 reduce-scatter.2.cloned.1.call-start
  7.3 63.3 %all-gather.4.cloned.1.call-done = bf16[3584,576]{1,0:T(8,128)(2,1)} async-done(((bf16[448,576]{1,0:T(8,128)(2,1)}), bf16[3584,576]{1,0:T(8,128)(2,1)}) %all-gather.4.cloned.1.call-update) | async-done | bytes 4128784 | tf_op jit(solution)/shard_map/all_gather | solution.py:25
  70.6 4.9 %convolution_bitcast_fusion = f32[448,1792]{1,0:T(8,128)} fusion(bf16[448,576]{1,0:T(8,128)(2,1)} %param.1, bf16[3584,576]{1,0:T(8,128)(2,1)} %all-gather.4.cloned.1.call-done, s32[]{:T(128)S(6)} %select_n.9), kind=kOutput, calls=%fused_computation.1 | convolution fusion | flops 924844032 | bytes 6078468 | tf_op jit(solution)/shard_map/dot_general | solution.py:20
  75.5 0.0 collective-permute-start
  75.5 6.0 %collective-permute-done = f32[448,1792]{1,0:T(8,128)S(1)} collective-permute-done((f32[448,1792]{1,0:T(8,128)}, f32[448,1792]{1,0:T(8,128)S(1)}, u32[]{:S(2)}, u32[]{:S(2)}) %collective-permute-start) | collective-permute-done | bytes 3211296 | tf_op jit(solution)/shard_map/ppermute | solution.py:29
  81.4 4.9 %bitcast_add_fusion = f32[448,1792]{1,0:T(8,128)} fusion(f32[448,1792]{1,0:T(8,128)S(1)} %collective-permute-done, bf16[448,576]{1,0:T(8,128)(2,1)} %param.1, bf16[3584,576]{1,0:T(8,128)(2,1)} %all-gather.4.cloned.1.call-done, s32[]{:T(128)S(6)} %select_n.8), kind=kOutput, calls=%fused_computation | convolution fusion | flops 925646848 | bytes 9289732 | tf_op jit(solution)/shard_map/dot_general | solution.py:20
  86.3 0.0 reduce-scatter.2.cloned.1.call-update
  86.3 0.0 all-gather.6.cloned.1.call-start
  86.4 45.2 %reduce-scatter.2.cloned.1.call-done = f32[56,1792]{1,0:T(8,128)} async-done(((f32[448,1792]{1,0:T(8,128)}), f32[56,1792]{1,0:T(8,128)}) %reduce-scatter.2.cloned.1.call-update) | async-done | bytes 401424 | tf_op jit(solution)/shard_map/reduce_scatter | solution.py:31
  131.6 3.0 %collective-permute-start.1 = (f32[56,1792]{1,0:T(8,128)}, f32[56,1792]{1,0:T(8,128)S(1)}, u32[]{:S(2)}, u32[]{:S(2)}) collective-permute-start(f32[56,1792]{1,0:T(8,128)} %reduce-scatter.2.cloned.1.call-done), channel_id=1, source_target_pairs={{0,16},{16,0},{1,17},{17,1},{2,18},{18,2},{3,19},{19,3},{4,20},{20... | collective-permute-start | bytes 1204232 | tf_op jit(solution)/shard_map/ppermute | solution.py:32
  134.6 7.1 %collective-permute-done.1 = f32[56,1792]{1,0:T(8,128)S(1)} collective-permute-done((f32[56,1792]{1,0:T(8,128)}, f32[56,1792]{1,0:T(8,128)S(1)}, u32[]{:S(2)}, u32[]{:S(2)}) %collective-permute-start.1) | collective-permute-done | bytes 401440 | tf_op jit(solution)/shard_map/ppermute | solution.py:32
  141.7 1.7 add_convert_fusion
  143.4 0.0 all-gather.6.cloned.1.call-update
  143.4 0.0 all-gather.8.cloned.1.call-start
  143.5 40.6 %all-gather.6.cloned.1.call-done = bf16[448,1792]{1,0:T(8,128)(2,1)} async-done(((bf16[56,1792]{1,0:T(8,128)(2,1)}), bf16[448,1792]{1,0:T(8,128)(2,1)}) %all-gather.6.cloned.1.call-update) | async-done | bytes 1605648 | tf_op jit(solution)/shard_map/all_gather | solution.py:33
  184.0 3.7 %collective-permute-done.2 = bf16[448,1792]{1,0:T(8,128)(2,1)S(1)} collective-permute-done((bf16[448,1792]{1,0:T(8,128)(2,1)}, bf16[448,1792]{1,0:T(8,128)(2,1)S(1)}, u32[]{:S(2)}, u32[]{:S(2)}) %collective-permute-start.2) | collective-permute-done | bytes 1605664 | tf_op jit(solution)/shard_map/ppermute | solution.py:34
  187.7 3.6 %fusion.4 = f32[448,576]{1,0:T(8,128)S(1)} fusion(bf16[448,1792]{1,0:T(8,128)(2,1)S(1)} %collective-permute-done.2, bf16[3584,576]{1,0:T(8,128)(2,1)} %all-gather.4.cloned.1.call-done, s32[]{:T(128)S(6)} %select_n.9), kind=kOutput, calls=%fused_computation.6 | convolution fusion | flops 924844032 | bytes 4931588 | tf_op jit(solution)/shard_map/dot_general | solution.py:20
  191.4 2.3 fusion.31
  193.7 0.0 all-gather.8.cloned.1.call-update
  193.7 0.0 copy-start
  193.7 57.9 %all-gather.8.cloned.1.call-done = bf16[3584,576]{1,0:T(8,128)(2,1)} async-done(((bf16[448,576]{1,0:T(8,128)(2,1)}), bf16[3584,576]{1,0:T(8,128)(2,1)}) %all-gather.8.cloned.1.call-update) | async-done | bytes 4128784 | tf_op jit(solution)/shard_map/all_gather | solution.py:36
  251.6 3.7 %fusion = f32[448,576]{1,0:T(8,128)S(1)} fusion(bf16[448,1792]{1,0:T(8,128)(2,1)} %copy-done.4, bf16[3584,576]{1,0:T(8,128)(2,1)} %all-gather.8.cloned.1.call-done, s32[]{:T(128)S(6)} %select_n.9), kind=kOutput, calls=%fused_computation.2 | convolution fusion | flops 924844032 | bytes 4931588 | tf_op jit(solution)/shard_map/dot_general | solution.py:20
  255.3 2.6 fusion.22
  (11 shorter events, 0.0 us)
Async XLA Ops:
  6.5 64.1 %all-gather.4.cloned.1.call-start = ((), (), s32[]{:S(2)}) async-start(), calls=%async_computation.1 | async-start | bytes 5160960 | tf_op jit(solution)/shard_map/all_gather | solution.py:25
  7.3 124.4 %reduce-scatter.2.cloned.1.call-start = ((), (), s32[]{:S(2)}) async-start(), calls=%async_computation.2 | async-start | bytes 3612672 | tf_op jit(solution)/shard_map/reduce_scatter | solution.py:31
  75.5 6.0 %collective-permute-start = (f32[448,1792]{1,0:T(8,128)}, f32[448,1792]{1,0:T(8,128)S(1)}, u32[]{:S(2)}, u32[]{:S(2)}) collective-permute-start(f32[448,1792]{1,0:T(8,128)} %convolution_bitcast_fusion), channel_id=1, source_target_pairs={{0,8},{8,0},{1,9},{9,1},{2,10},{10,2},{3,11},{11,3},{4,12},{12,4},... | collective-permute-start | bytes 9633800 | tf_op jit(solution)/shard_map/ppermute | solution.py:29
  86.3 97.7 %all-gather.6.cloned.1.call-start = ((), (), s32[]{:S(2)}) async-start(), calls=%async_computation.3 | async-start | bytes 1806336 | tf_op jit(solution)/shard_map/all_gather | solution.py:33
  131.6 10.0 %collective-permute-start.1 = (f32[56,1792]{1,0:T(8,128)}, f32[56,1792]{1,0:T(8,128)S(1)}, u32[]{:S(2)}, u32[]{:S(2)}) collective-permute-start(f32[56,1792]{1,0:T(8,128)} %reduce-scatter.2.cloned.1.call-done), channel_id=1, source_target_pairs={{0,16},{16,0},{1,17},{17,1},{2,18},{18,2},{3,19},{19,3},{4,20},{20... | collective-permute-start | bytes 1204232 | tf_op jit(solution)/shard_map/ppermute | solution.py:32
  143.4 108.2 %all-gather.8.cloned.1.call-start = ((), (), s32[]{:S(2)}) async-start(), calls=%async_computation.4 | async-start | bytes 5160960 | tf_op jit(solution)/shard_map/all_gather | solution.py:36
  184.0 7.3 %copy-start.1 = (bf16[3584,576]{1,0:T(8,128)(2,1)S(1)}, bf16[3584,576]{1,0:T(8,128)(2,1)}, u32[]{:S(2)}) copy-start(bf16[3584,576]{1,0:T(8,128)(2,1)} %all-gather.4.cloned.1.call-done) | copy-start | bytes 12386308
  184.0 7.3 %copy-start.3 = (bf16[448,1792]{1,0:T(8,128)(2,1)S(1)}, bf16[448,1792]{1,0:T(8,128)(2,1)}, u32[]{:S(2)}) copy-start(bf16[448,1792]{1,0:T(8,128)(2,1)} %all-gather.6.cloned.1.call-done) | copy-start | bytes 4816900
  184.0 3.7 %collective-permute-start.2 = (bf16[448,1792]{1,0:T(8,128)(2,1)}, bf16[448,1792]{1,0:T(8,128)(2,1)S(1)}, u32[]{:S(2)}, u32[]{:S(2)}) collective-permute-start(bf16[448,1792]{1,0:T(8,128)(2,1)} %all-gather.6.cloned.1.call-done), channel_id=1, source_target_pairs={{0,8},{8,0},{1,9},{9,1},{2,10},{10,2},{3,11},{11,3},{4,12},{12,4},... | collective-permute-start | bytes 4816904 | tf_op jit(solution)/shard_map/ppermute | solution.py:34
  187.7 3.6 %copy-start.4 = (bf16[448,1792]{1,0:T(8,128)(2,1)}, bf16[448,1792]{1,0:T(8,128)(2,1)S(1)}, u32[]{:S(2)}) copy-start(bf16[448,1792]{1,0:T(8,128)(2,1)S(1)} %collective-permute-done.2) | copy-start | bytes 4816900
  193.7 61.6 %copy-start = (bf16[448,576]{1,0:T(8,128)(2,1)S(1)}, bf16[448,576]{1,0:T(8,128)(2,1)}, u32[]{:S(2)}) copy-start(bf16[448,576]{1,0:T(8,128)(2,1)} %param.1) | copy-start | bytes 1548292
  251.6 3.7 %copy-start.2 = (bf16[3584,576]{1,0:T(8,128)(2,1)S(1)}, bf16[3584,576]{1,0:T(8,128)(2,1)}, u32[]{:S(2)}) copy-start(bf16[3584,576]{1,0:T(8,128)(2,1)} %all-gather.8.cloned.1.call-done) | copy-start | bytes 12386308
Sparse Core Ops, SparseCore 0:
  9.1 61.4 all-gather.3
  86.4 45.1 reduce-scatter.1
  143.5 40.4 all-gather.5
  193.8 57.7 all-gather.7
